TPU v7x, 32 devices: a whole 2x2x4 slice. The times are simulated.
32 devices in a mesh: blocks: 8 (over z, core), lev: 4 (over y, x).
Axes of the slice: x: 2, y: 2, z: 4, core: 2. Of those that a mesh axis runs over, the one named last changes fastest.
Arguments:
- tracers: float32 [8, 4, 8, 128, 128], P('blocks', 'lev'), may hold values from -6 to 6
- east_velocity: float32 [8, 8, 128, 128], P('blocks'), may hold values from -0.24 to 0.24
- north_velocity: float32 [8, 8, 128, 128], P('blocks'), may hold values from -0.24 to 0.24
- upward_velocity: float32 [8, 8, 128, 128], P('blocks'), may hold values from -0.24 to 0.24
- target: float32 [8, 4, 8, 128, 128], P('blocks', 'lev'), may hold values from 0.09375 to 12.65625
- bottom: int32 [8, 128, 128], P('blocks'), may hold values from 0 to 8, as said below
- shave_fraction: float32 [8, 128, 128], P('blocks'), may hold values from 0.05 to 1, as said below
- side_bottom: int32 [8, 4, 128], P('blocks'), may hold values from 0 to 8, as said below
- neighbors: int32 [8, 4], P('blocks'), may hold values from -1 to 7, as said below
- fold_partner: int32 [8], P('blocks'), may hold values from -1 to 7, as said below
- thin_pairs: int32 [8, 2, 128], P('blocks'), may hold values from 0 to 16383, as said below
Outputs:
- new_tracers: float32 [8, 4, 8, 128, 128], P('blocks', 'lev')
Inputs may be any that keep to these rules, and one draw needn't show every extreme that they name: The blocks form a grid of 3 block columns, periodic from west to east, and 4 block rows; entries are mutual: neighbors[b,0] = c exactly when neighbors[c,1] = b, and neighbors[b,2] = c exactly when neighbors[c,3] = b; a block's entries that are not -1 differ; blocks of the top row have -1 to the north. `fold_partner`: set exactly for the blocks of the top row; mutual, a block may be its own partner. `bottom`: every block has wet columns. `side_bottom`: equals the bottom of the adjacent column or row of the neighbouring block, across the north fold the partner's top row in reversed order, 0 where no block lies. `thin_pairs`: thin cells of a block are distinct and have bottom 1 or more; each partner is the cell just east of its thin cell in the same row, with a bottom no smaller; no cell appears twice in a block. `shave_fraction`: listed thin cells have 0.05 to 0.2, all other cells 0.5 to 1.
All inputs are finite; a program needn't handle non-finite values.
Results may differ from a plain program's by a relative error of at most 0.0003.
Values sent between devices are 32-bit elements; how exact they have to be, the bound alone decides.
A program may use at most 64 MiB of HBM per device.

v0:
```python
import jax
import jax.numpy as jnp
from jax import lax
from jax.sharding import PartitionSpec as P

RATE = 0.5
facing_order = (1, 0, 3, 2)


def upwind(face, first, second):
    return jnp.maximum(face, 0.0) * first + jnp.minimum(face, 0.0) * second


def column_masks(levels, bottom, shave_fraction):
    level_grid = levels[None, None, :, None, None]
    column_bottom = bottom[:, None, None]
    wet = level_grid < column_bottom
    thick = jnp.where(
        level_grid < column_bottom - 1,
        1.0,
        jnp.where(level_grid == column_bottom - 1, shave_fraction[:, None, None], 0.0),
    )
    return (wet, thick)


def level_pair(field):
    zero_level = jnp.zeros_like(field[:, :, :1])
    return (
        jnp.concatenate([zero_level, field[:, :, :-1]], 2),
        jnp.concatenate([field[:, :, 1:], zero_level], 2),
    )


def advected_field(
    tracers,
    east_flow,
    north_flow,
    upward_flow,
    levels,
    bottom,
    wet,
    thick,
    side_bottom,
    west_pair,
    east_pair,
    south_pair,
    north_pair,
):
    level_grid = levels[None, None, :, None, None]
    column_bottom = bottom[:, None, None]
    edge_levels = levels[None, None, :, None]
    wet_west = edge_levels < side_bottom[:, 0][:, None, None, :]
    wet_east = edge_levels < side_bottom[:, 1][:, None, None, :]
    wet_south = edge_levels < side_bottom[:, 2][:, None, None, :]
    wet_north = edge_levels < side_bottom[:, 3][:, None, None, :]
    east_values = jnp.concatenate([tracers[..., 1:], east_pair[0][..., None]], -1)
    east_flows = jnp.concatenate([east_flow[..., 1:], east_pair[1][..., None]], -1)
    east_wets = jnp.concatenate([wet[..., 1:], wet_east[..., None]], -1)
    flux_east = upwind(
        jnp.where(wet & east_wets, 0.5 * (east_flow + east_flows), 0.0), tracers, east_values
    )
    west_face = jnp.where(wet_west & wet[..., 0], 0.5 * (west_pair[1] + east_flow[..., 0]), 0.0)
    flux_west = jnp.concatenate(
        [upwind(west_face, west_pair[0], tracers[..., 0])[..., None], flux_east[..., :-1]], -1
    )
    north_values = jnp.concatenate([tracers[..., 1:, :], north_pair[0][..., None, :]], -2)
    north_flows = jnp.concatenate([north_flow[..., 1:, :], north_pair[1][..., None, :]], -2)
    north_wets = jnp.concatenate([wet[..., 1:, :], wet_north[..., None, :]], -2)
    flux_north = upwind(
        jnp.where(wet & north_wets, 0.5 * (north_flow + north_flows), 0.0), tracers, north_values
    )
    south_face = jnp.where(
        wet_south & wet[..., 0, :], 0.5 * (south_pair[1] + north_flow[..., 0, :]), 0.0
    )
    flux_south = jnp.concatenate(
        [
            upwind(south_face, south_pair[0], tracers[..., 0, :])[..., None, :],
            flux_north[..., :-1, :],
        ],
        -2,
    )
    above_values, below_values = level_pair(tracers)
    above_flow, below_flow = level_pair(upward_flow)
    wet_above = (level_grid >= 1) & (level_grid - 1 < column_bottom)
    wet_below = level_grid + 1 < column_bottom
    flux_lower = upwind(
        jnp.where(wet & wet_below, 0.5 * (upward_flow + below_flow), 0.0), below_values, tracers
    )
    flux_upper = upwind(
        jnp.where(wet & wet_above, 0.5 * (above_flow + upward_flow), 0.0), tracers, above_values
    )
    divergence = flux_west - flux_east + flux_south - flux_north + flux_lower - flux_upper
    return tracers + jnp.where(wet, divergence / jnp.where(wet, thick, 1.0), 0.0)


def merge_block(field, bottom, shave_fraction, pairs, levels):
    flat = field.reshape(field.shape[0], field.shape[1], -1)
    thin_cells = pairs[0]
    partner = pairs[1]
    depth_index = bottom[thin_cells] - 1
    thin_thick = shave_fraction[thin_cells]
    partner_thick = jnp.where(bottom[partner] - 1 == depth_index, shave_fraction[partner], 1.0)
    thin_values = flat[:, :, thin_cells]
    partner_values = flat[:, :, partner]
    merged = (thin_thick * thin_values + partner_thick * partner_values) / (
        thin_thick + partner_thick
    )
    struck = levels[:, None] == depth_index[None, :]
    flat = flat.at[:, :, thin_cells].set(jnp.where(struck, merged, thin_values))
    flat = flat.at[:, :, partner].set(jnp.where(struck, merged, partner_values))
    return flat.reshape(field.shape)


def local(
    tracers,
    east_velocity,
    north_velocity,
    upward_velocity,
    target,
    bottom,
    shave_fraction,
    side_bottom,
    neighbors,
    fold_partner,
    thin_pairs,
):
    blocks_here, tracer_count, level_count, cells_side, _ = tracers.shape
    levels = jnp.arange(level_count, dtype=jnp.int32)
    east_flow = east_velocity[:, None]
    north_flow = north_velocity[:, None]
    upward_flow = upward_velocity[:, None]
    wet, thick = column_masks(levels, bottom, shave_fraction)
    restoring = RATE * (target - tracers)
    tracer_edges = jnp.stack(
        [
            tracers[..., 0],
            tracers[..., cells_side - 1],
            tracers[..., 0, :],
            tracers[..., cells_side - 1, :],
        ],
        1,
    )
    flow_edges = jnp.stack(
        [
            east_velocity[..., 0],
            east_velocity[..., cells_side - 1],
            north_velocity[..., 0, :],
            north_velocity[..., cells_side - 1, :],
        ],
        1,
    )
    tracer_piece = lax.all_gather(tracer_edges, "blocks", axis=0, tiled=True)
    flow_piece = lax.all_gather(flow_edges, "blocks", axis=0, tiled=True)
    owners = jnp.arange(tracer_piece.shape[0], dtype=jnp.int32)
    side_match = (neighbors[:, :, None] == owners[None, None, :]).astype(jnp.float32)
    fold_match = (fold_partner[:, None] == owners[None, :]).astype(jnp.float32)
    tracer_facing = jnp.stack([tracer_piece[:, side] for side in facing_order], 1)
    flow_facing = jnp.stack([flow_piece[:, side] for side in facing_order], 1)
    highest = lax.Precision.HIGHEST
    tracer_sides = jnp.einsum("bsq,qstlc->bstlc", side_match, tracer_facing, precision=highest)
    flow_sides = jnp.einsum("bsq,qslc->bslc", side_match, flow_facing, precision=highest)
    tracer_fold = jnp.einsum("bq,qtlc->btlc", fold_match, tracer_piece[:, 3], precision=highest)
    flow_fold = jnp.einsum("bq,qlc->blc", fold_match, flow_piece[:, 3], precision=highest)
    tracer_sides, flow_sides, tracer_fold, flow_fold = (
        tracer_sides,
        flow_sides,
        tracer_fold,
        flow_fold,
    )
    west_pair = (tracer_sides[:, 0], flow_sides[:, 0][:, None])
    east_pair = (tracer_sides[:, 1], flow_sides[:, 1][:, None])
    south_pair = (tracer_sides[:, 2], flow_sides[:, 2][:, None])
    north_pair = (
        tracer_sides[:, 3] + tracer_fold[..., ::-1],
        (flow_sides[:, 3] - flow_fold[..., ::-1])[:, None],
    )
    advected = advected_field(
        tracers,
        east_flow,
        north_flow,
        upward_flow,
        levels,
        bottom,
        wet,
        thick,
        side_bottom,
        west_pair,
        east_pair,
        south_pair,
        north_pair,
    )
    source_part = jnp.sum(jnp.where(wet, thick * restoring, 0.0))
    volume_part = tracer_count * jnp.sum(jnp.where(wet, thick, 0.0))
    total_source, total_volume = lax.psum((source_part, volume_part), ("blocks", "lev"))
    stepped = jnp.where(wet, advected + restoring - total_source / total_volume, 0.0)
    return jax.vmap(merge_block, in_axes=(0, 0, 0, 0, None))(
        stepped,
        bottom.reshape(blocks_here, -1),
        shave_fraction.reshape(blocks_here, -1),
        thin_pairs,
        levels,
    )


def solution(mesh):
    placed = (
        P("blocks", "lev", None, None, None),
        P("blocks", None, None, None),
        P("blocks", None, None, None),
        P("blocks", None, None, None),
        P("blocks", "lev", None, None, None),
        P("blocks", None, None),
        P("blocks", None, None),
        P("blocks", None, None),
        P("blocks", None),
        P("blocks"),
        P("blocks", None, None),
    )
    return jax.shard_map(
        local,
        mesh=mesh,
        in_specs=placed,
        out_specs=P("blocks", "lev", None, None, None),
        check_vma=False,
    )
```

profile of v0, /device:TPU:0, one launch (start us, length us, event | category | flops | bytes accessed | tf_op | source)
XLA Modules:
  0.0 142.8 jit_solution(14295205948113703087)
XLA Ops:
  2.0 0.8 compare_select_fusion
  3.4 1.8 %gather_fusion.4 = f32[128]{0:T(128)S(1)} fusion(f32[1,16384]{1,0:T(1,128)} %bitcast.215, s32[128]{0:T(128)S(1)} %get-tuple-element.43), kind=kCustom, calls=%fused_computation.4 | custom fusion | bytes 2048 | tf_op jit(solution)/shard_map/vmap()/gather | solution.py:102
  5.1 1.8 %gather_fusion.3 = s32[128]{0:T(128)S(1)} fusion(s32[1,16384]{1,0:T(1,128)} %bitcast.212, s32[128]{0:T(128)S(1)} %get-tuple-element.43), kind=kCustom, calls=%fused_computation.3 | custom fusion | bytes 2048 | tf_op jit(solution)/shard_map/vmap()/gather | solution.py:102
  7.5 1.8 %gather_fusion.1 = f32[128]{0:T(128)S(1)} fusion(f32[1,16384]{1,0:T(1,128)} %bitcast.216, s32[128]{0:T(128)S(1)} %get-tuple-element.46), kind=kCustom, calls=%fused_computation.1 | custom fusion | bytes 2048 | tf_op jit(solution)/shard_map/vmap()/gather | solution.py:101
  9.2 1.8 %gather_fusion = s32[128]{0:T(128)S(1)} fusion(s32[1,16384]{1,0:T(1,128)} %bitcast.213, s32[128]{0:T(128)S(1)} %get-tuple-element.46), kind=kCustom, calls=%fused_computation | custom fusion | bytes 2048 | tf_op jit(solution)/shard_map/vmap()/gather | solution.py:100
  11.6 1.4 slice_bitcast_fusion.15
  13.5 0.8 fusion.78
  14.3 0.8 fusion.77
  15.1 0.9 copy.208
  16.0 0.9 copy.235
  16.9 0.9 broadcast_add_fusion
  19.2 0.9 slice.230
  20.0 1.3 copy.236
  21.3 15.7 %all_gather.7 = f32[8,4,1,8,128]{4,3,2,1,0:T(8,128)S(1)} all-gather(f32[1,4,1,8,128]{4,3,2,1,0:T(8,128)S(1)} %pad_maximum_fusion.2), channel_id=1, replica_groups=mesh['blocks'=8,'lev'=4] {'blocks'}, dimensions={0}, use_global_device_ids=true | all-gather | bytes 147456 | tf_op jit(solution)/shard_map/all_gather | solution.py:152
  37.6 1.0 copy.227
  38.6 0.8 slice.223
  39.5 1.3 copy.209
  40.8 14.0 %all_gather.6 = f32[8,4,8,128]{3,2,1,0:T(8,128)S(1)} all-gather(f32[1,4,8,128]{3,2,1,0:T(8,128)S(1)} %pad_maximum_fusion.1), channel_id=1, replica_groups=mesh['blocks'=8,'lev'=4] {'blocks'}, dimensions={0}, use_global_device_ids=true | all-gather | bytes 147456 | tf_op jit(solution)/shard_map/all_gather | solution.py:153
  55.3 1.0 copy.224
  56.3 0.8 slice.221
  57.6 1.3 copy.221
  59.8 1.0 copy.228
  61.3 4.0 %select_reduce_fusion = (f32[]{:T(128)}, f32[]{:T(128)}, f32[1,1,8,128,128]{3,2,4,1,0:T(8,128)}, f32[1,1,8,128,128]{3,2,4,1,0:T(8,128)S(1)}) fusion(f32[128,128]{0,1:T(8,128)S(1)} %copy.235, s32[128,128]{0,1:T(8,128)S(1)} %copy.234, s32[128,128]{0,1:T(8,128)S(1)} %copy.208, f32[1,1,8,128,128]{3,2,4,1,0:T(8,128)S(1)} %copy.237, ...), kind=kLoop, calls=%fused_computation.28 | loop fusion | flops 4718590 | bytes 5701640 | tf_op jit(solution)/shard_map/reduce_sum | solution.py:193
  65.3 40.5 %all-reduce.4 = (f32[]{:T(128)}, f32[]{:T(128)}) all-reduce(f32[]{:T(128)} %get-tuple-element.6, f32[]{:T(128)} %get-tuple-element.5), channel_id=1, replica_groups=mesh['blocks'=8,'lev'=4] {'blocks','lev'}, use_global_device_ids=true, to_apply=%region_1.2 | all-reduce | flops 2 | bytes 16 | tf_op jit(solution)/shard_map/psum | solution.py:194
  107.1 1.1 slice.225
  108.3 2.3 %subtract_select_fusion = f32[1,1,8,128,128]{3,2,4,1,0:T(8,128)S(1)} fusion(f32[1,1,8,128,128]{3,2,4,1,0:T(8,128)S(1)} %copy.236, f32[1,1,8,128,128]{3,2,4,1,0:T(8,128)S(1)} %get-tuple-element.12, f32[1,1,8,127,128]{3,2,4,1,0:T(8,128)S(1)} %bitcast.223, f32[1,1,8,1,128]{3,2,4,1,0:T(8,128)} %copy.228, f32[1,1,8,128,128]{3,2,4,1,0:T(8,128)} %get-tuple-element.11, ...), kind=kLoop, calls=%fused_computation.27 | loop fusion | flops 5505024 | bytes 6225996 | tf_op jit(solution)/shard_map/jit(_where)/select_n | solution.py:195
  110.6 7.4 %copy.239 = f32[1,1,8,128,128]{2,4,3,1,0:T(8,128)} copy(f32[1,1,8,128,128]{3,2,4,1,0:T(8,128)S(1)} %subtract_select_fusion) | data formatting | bytes 1048576 | tf_op jit(solution)/shard_map/jit(_where)/select_n | solution.py:195
  118.0 1.8 %gather_fusion.5 = f32[128,8]{1,0:T(8,128)S(1)} fusion(f32[1,8,16384]{1,2,0:T(8,128)} %bitcast.208, s32[128]{0:T(128)S(1)} %get-tuple-element.43), kind=kCustom, calls=%fused_computation.5 | custom fusion | bytes 9216 | tf_op jit(solution)/shard_map/vmap()/gather | solution.py:104
  119.8 1.8 %gather_fusion.2 = f32[128,8]{1,0:T(8,128)S(1)} fusion(f32[1,8,16384]{1,2,0:T(8,128)} %bitcast.209, s32[128]{0:T(128)S(1)} %get-tuple-element.46), kind=kCustom, calls=%fused_computation.2 | custom fusion | bytes 9216 | tf_op jit(solution)/shard_map/vmap()/gather | solution.py:103
  121.6 7.7 %scatter_custom_fusion = f32[8,16384]{0,1:T(8,128)} fusion(f32[8,16384]{0,1:T(8,128)} %bitcast.210, s32[128]{0:T(128)} %get-tuple-element.47, f32[128,8]{1,0:T(8,128)S(1)} %gather_fusion.2, f32[128,8]{1,0:T(8,128)S(1)} %gather_fusion.5, f32[128]{0:T(128)S(1)} %gather_fusion.1, s32[128]{0:T(128)S(1)} %broadcast_add_fusion.1, f32[128]{0:T(128)S(1)} %get-tuple-element.9, ...), kind=kCustom, calls=%fused_computation.47 | custom fusion | flops 6144 | bytes 534528 | tf_op jit(solution)/shard_map/vmap()/scatter | solution.py:109
  129.3 7.7 %scatter_custom_fusion.1 = f32[8,16384]{0,1:T(8,128)} fusion(f32[8,16384]{0,1:T(8,128)} %scatter_custom_fusion, s32[128]{0:T(128)} %get-tuple-element.42, f32[128,8]{1,0:T(8,128)S(1)} %gather_fusion.5, f32[128,8]{1,0:T(8,128)S(1)} %gather_fusion.2, f32[128]{0:T(128)S(1)} %gather_fusion.1, s32[128]{0:T(128)S(1)} %broadcast_add_fusion.1, ...), kind=kCustom, calls=%fused_computation.45 | custom fusion | flops 6144 | bytes 534528 | tf_op jit(solution)/shard_map/vmap()/scatter | solution.py:110
  136.9 5.9 %copy.241 = f32[1,1,8,128,128]{4,3,2,1,0:T(8,128)} copy(f32[1,1,8,128,128]{2,4,3,1,0:T(8,128)} %bitcast.211) | data formatting | bytes 1048576 | tf_op jit(solution)/shard_map/vmap()/reshape | solution.py:111
  (43 shorter events, 7.8 us)
Async XLA Ops:
  0.0 57.4 %copy-start.1 = (f32[1,1,8,128,128]{4,3,2,1,0:T(8,128)S(1)}, f32[1,1,8,128,128]{4,3,2,1,0:T(8,128)}, u32[]{:S(2)}) copy-start(f32[1,1,8,128,128]{4,3,2,1,0:T(8,128)} %param.15) | copy-start | bytes 1572868
  0.0 57.2 %copy-start = (f32[1,8,128,128]{3,2,1,0:T(8,128)S(1)}, f32[1,8,128,128]{3,2,1,0:T(8,128)}, u32[]{:S(2)}) copy-start(f32[1,8,128,128]{3,2,1,0:T(8,128)} %param.14) | copy-start | bytes 1572868
where the time goes:
time: 144 us; the launch traced here: 143 us
  blocking collectives  70.2 us (49%)
  local copies, waits for them, and re-layouts  41.9 us (29%)
  other arithmetic  27.6 us (19%)
  between operations  2.28 us (2%)
    psum x1, blocking collectives, local(): lax.psum((source_part, volume_part), ('blocks', 'lev'))  40.5 us
    all_gather x1, blocking collectives, local(): tracer_piece = lax.all_gather(tracer_edges, 'blocks', axis=0, tiled=True)  15.7 us
    all_gather x1, blocking collectives, local(): flow_piece = lax.all_gather(flow_edges, 'blocks', axis=0, tiled=True)  14 us
    scatter x2, other arithmetic, merge_block(): flat = flat.at[:, :, thin_cells].set(jnp.where(struck, merged, thin_values))  8.27 us
    scatter x1, other arithmetic, merge_block(): flat = flat.at[:, :, partner].set(jnp.where(struck, merged, partner_values))  7.68 us
    select_n x1, local copies, waits for them, and re-layouts, local(): jnp.where(wet, advected + restoring - total_source / total_volume, 0.0)  7.4 us
    reshape x1, local copies, waits for them, and re-layouts, merge_block(): return flat.reshape(field.shape)  5.85 us
    unnamed x9, local copies, waits for them, and re-layouts  4.29 us

commit v1 on v0

--- a/solution.py
+++ b/solution.py
@@ -5,6 +5,27 @@
 
 RATE = 0.5
 facing_order = (1, 0, 3, 2)
+
+
+def ring_gather(x, axis, dim):
+    count, place, extent = (lax.axis_size(axis), lax.axis_index(axis), x.shape[dim])
+    upward = [(i, (i + 1) % count) for i in range(count)]
+    left = [(i, (i - 1) % count) for i in range(count)]
+    out = jnp.zeros((*x.shape[:dim], count * extent, *x.shape[dim + 1 :]), x.dtype)
+    out = lax.dynamic_update_slice_in_dim(out, x, place * extent, axis=dim)
+    from_left = from_right = x
+    half = count // 2
+    for step in range(1, half + 1):
+        from_left = lax.ppermute(from_left, axis, upward)
+        out = lax.dynamic_update_slice_in_dim(
+            out, from_left, (place - step) % count * extent, axis=dim
+        )
+        if step < count - half:
+            from_right = lax.ppermute(from_right, axis, left)
+            out = lax.dynamic_update_slice_in_dim(
+                out, from_right, (place + step) % count * extent, axis=dim
+            )
+    return out
 
 
 def upwind(face, first, second):
@@ -149,7 +170,7 @@
         ],
         1,
     )
-    tracer_piece = lax.all_gather(tracer_edges, "blocks", axis=0, tiled=True)
+    tracer_piece = ring_gather(tracer_edges, "blocks", 0)
     flow_piece = lax.all_gather(flow_edges, "blocks", axis=0, tiled=True)
     owners = jnp.arange(tracer_piece.shape[0], dtype=jnp.int32)
     side_match = (neighbors[:, :, None] == owners[None, None, :]).astype(jnp.float32)

time: 144 us -> 155 us (1.076)
  blocking collectives: 70.2 us -> 52.5 us
  starting transfers between devices: 0 us -> 11.6 us
  other arithmetic: 27.6 us -> 35 us
  local copies, waits for them, and re-layouts: 41.9 us -> 46.6 us
  waiting for transfers between devices: 0 us -> 3.98 us
    all_gather x1 -> x0, blocking collectives: 15.7 us -> none  [local(): tracer_piece = lax.all_gather(tracer_edges, 'blocks', axis=0, tiled=True)]
    ppermute x0 -> x7, starting transfers between devices: none -> 11.6 us  [the longest x3 10.8 us: ring_gather(): from_right = lax.ppermute(from_right, axis, left)]
    dynamic_update_slice x0 -> x7, local copies, waits for them, and re-layouts: none -> 5.63 us  [the longest x4 3.11 us: ring_gather(): lax.dynamic_update_slice_in_dim(out, from_left, (place - step) % count *...]
    add x0 -> x4, other arithmetic: none -> 4.35 us  [the longest x1 2.19 us: advected_field(): north_flow + north_flows]
    ppermute x0 -> x7, waiting for transfers between devices: none -> 3.98 us  [the longest x4 3.97 us: ring_gather(): from_left = lax.ppermute(from_left, axis, upward)]
    select_n x1, local copies, waits for them, and re-layouts: 7.4 us -> 4.63 us  [local(): jnp.where(wet, advected + restoring - total_source / total_volume, 0.0)]
    slice x1, local copies, waits for them, and re-layouts: 0.14 us -> 2.74 us  [level_pair(): field[:, :, 1:]]
    concatenate x2 -> x0, local copies, waits for them, and re-layouts: 2.07 us -> none  [the longest x1 1.04 us: advected_field(): jnp.concatenate([north_flow[..., 1:, :], north_pair[1][..., None, :]], -2)]
  transfers between devices with their start and end apart: 0 -> 7, of which waited for: 0 -> 2; matrix products, arithmetic and copies ran while one was open for 0% -> 26% of each run, Pallas kernels for 0% -> 0%
where the time goes in v1:
time: 155 us; the launch traced here: 153 us
  blocking collectives  52.5 us (34%)
  local copies, waits for them, and re-layouts  46.6 us (30%)
  other arithmetic  35 us (23%)
  starting transfers between devices  11.6 us (7%)
  waiting for transfers between devices  3.98 us (3%)
  between operations  2.33 us (2%)
    psum x1, blocking collectives, local(): lax.psum((source_part, volume_part), ('blocks', 'lev'))  38.6 us
    all_gather x1, blocking collectives, local(): flow_piece = lax.all_gather(flow_edges, 'blocks', axis=0, tiled=True)  14 us
    ppermute x3, starting transfers between devices, ring_gather(): from_right = lax.ppermute(from_right, axis, left)  10.8 us
    scatter x2, other arithmetic, merge_block(): flat = flat.at[:, :, thin_cells].set(jnp.where(struck, merged, thin_values))  8.27 us
    scatter x1, other arithmetic, merge_block(): flat = flat.at[:, :, partner].set(jnp.where(struck, merged, partner_values))  7.73 us
    reshape x1, local copies, waits for them, and re-layouts, merge_block(): return flat.reshape(field.shape)  5.85 us
    select_n x1, local copies, waits for them, and re-layouts, local(): jnp.where(wet, advected + restoring - total_source / total_volume, 0.0)  4.63 us
    unnamed x33, local copies, waits for them, and re-layouts  4.54 us
  transfers between devices with their start and end apart: 7, of which 2 were waited for; matrix products, arithmetic and copies ran while one was open for 26% of the time, Pallas kernels for 0%

profile of v1, /device:TPU:0, one launch (start us, length us, event | category | flops | bytes accessed | tf_op | source)
XLA Modules:
  0.0 152.9 jit_solution(7835337994728739838)
XLA Ops:
  0.0 0.9 fusion.73
  0.9 1.3 copy.69
  3.3 4.0 %collective-permute-start.1 = (f32[1,4,1,8,128]{4,3,2,1,0:T(8,128)}, f32[1,4,1,8,128]{4,3,2,1,0:T(8,128)}, u32[]{:S(2)}, u32[]{:S(2)}) collective-permute-start(f32[1,4,1,8,128]{4,3,2,1,0:T(8,128)} %get-tuple-element.39), channel_id=1, source_target_pairs={{0,28},{4,0},{8,4},{12,8},{16,12},{20,16},{24,20},{28,24},{1,29},{... | collective-permute-start | bytes 49160 | tf_op jit(solution)/shard_map/ppermute | solution.py:24
  8.7 2.3 %gather_fusion.4 = f32[128]{0:T(128)} fusion(f32[1,16384]{1,0:T(1,128)} %bitcast.219, s32[128]{0:T(128)S(1)} %get-tuple-element.46), kind=kCustom, calls=%fused_computation.4 | custom fusion | bytes 2048 | tf_op jit(solution)/shard_map/vmap()/gather | solution.py:123
  11.0 2.3 %gather_fusion.3 = s32[128]{0:T(128)} fusion(s32[1,16384]{1,0:T(1,128)} %bitcast.214, s32[128]{0:T(128)S(1)} %get-tuple-element.46), kind=kCustom, calls=%fused_computation.3 | custom fusion | bytes 2048 | tf_op jit(solution)/shard_map/vmap()/gather | solution.py:123
  13.8 2.4 %gather_fusion.1 = f32[128]{0:T(128)} fusion(f32[1,16384]{1,0:T(1,128)} %bitcast.220, s32[128]{0:T(128)S(1)} %get-tuple-element.49), kind=kCustom, calls=%fused_computation.1 | custom fusion | bytes 2048 | tf_op jit(solution)/shard_map/vmap()/gather | solution.py:122
  16.2 1.8 %gather_fusion = s32[128]{0:T(128)S(1)} fusion(s32[1,16384]{1,0:T(1,128)} %bitcast.215, s32[128]{0:T(128)S(1)} %get-tuple-element.49), kind=kCustom, calls=%fused_computation | custom fusion | bytes 2048 | tf_op jit(solution)/shard_map/vmap()/gather | solution.py:121
  18.5 1.5 broadcast_add_fusion
  21.8 1.4 slice_bitcast_fusion.16
  24.4 0.9 iota_compare_fusion.2
  25.3 1.3 copy.64
  26.6 1.4 copy.131
  27.9 14.0 %all_gather.3 = f32[8,4,8,128]{3,2,1,0:T(8,128)S(1)} all-gather(f32[1,4,8,128]{3,2,1,0:T(8,128)S(1)} %pad_maximum_fusion.1), channel_id=1, replica_groups=mesh['blocks'=8,'lev'=4] {'blocks'}, dimensions={0}, use_global_device_ids=true | all-gather | bytes 147456 | tf_op jit(solution)/shard_map/all_gather | solution.py:174
  43.6 2.7 %fusion.71 = (f32[1,1,7,128,128]{4,3,2,1,0:T(8,128)}, f32[1,1,7,128,128]{4,3,2,1,0:T(8,128)}, f32[1,1,7,128,128]{4,3,2,1,0:T(8,128)}, f32[1,1,7,128,128]{4,3,2,1,0:T(8,128)}) fusion(f32[1,1,8,128,128]{4,3,2,1,0:T(8,128)} %bitcast.226, f32[1,1,8,128,128]{4,3,2,1,0:T(8,128)} %param.11), kind=kLoop, calls=%fused_computation.153 | loop fusion | bytes 3670016 | tf_op jit(solution)/shard_map/slice | solution.py:51
  47.8 2.2 %maximum_add_fusion.1 = f32[1,1,8,128,128]{4,2,3,1,0:T(8,128)} fusion(f32[1,1,8,1,128]{4,2,3,1,0:T(8,128)S(1)} %fusion.43, f32[1,1,8,127,128]{4,2,3,1,0:T(8,128)} %slice.233, f32[1,8,128,128]{3,2,1,0:T(8,128)S(1)} %copy-done.4), kind=kLoop, calls=%fused_computation.14 | loop fusion | flops 262144 | bytes 1572864 | tf_op jit(solution)/shard_map/add | solution.py:91
  50.0 1.3 fusion.70
  55.2 1.3 copy.83
  58.3 3.2 %collective-permute-start.3 = (f32[1,4,1,8,128]{4,3,2,1,0:T(8,128)}, f32[1,4,1,8,128]{4,3,2,1,0:T(8,128)S(1)}, u32[]{:S(2)}, u32[]{:S(2)}) collective-permute-start(f32[1,4,1,8,128]{4,3,2,1,0:T(8,128)} %collective-permute-done.1), channel_id=1, source_target_pairs={{0,28},{4,0},{8,4},{12,8},{16,12},{20,16},{24,20},{28,24},{1,29},{... | collective-permute-start | bytes 49160 | tf_op jit(solution)/shard_map/ppermute | solution.py:24
  61.5 1.3 constant_dynamic-update-slice_fusion.6
  62.8 1.3 constant_dynamic-update-slice_fusion.5
  64.1 3.5 %collective-permute-start.5 = (f32[1,4,1,8,128]{4,3,2,1,0:T(8,128)S(1)}, f32[1,4,1,8,128]{4,3,2,1,0:T(8,128)S(1)}, u32[]{:S(2)}, u32[]{:S(2)}) collective-permute-start(f32[1,4,1,8,128]{4,3,2,1,0:T(8,128)S(1)} %collective-permute-done.3), channel_id=1, source_target_pairs={{0,28},{4,0},{8,4},{12,8},{16,12},{20,16},{24,20},{28,24},{1,29},{... | collective-permute-start | bytes 49160 | tf_op jit(solution)/shard_map/ppermute | solution.py:24
  70.3 3.7 %collective-permute-done.6 = f32[1,4,1,8,128]{4,3,2,1,0:T(8,128)S(1)} collective-permute-done((f32[1,4,1,8,128]{4,3,2,1,0:T(8,128)S(1)}, f32[1,4,1,8,128]{4,3,2,1,0:T(8,128)S(1)}, u32[]{:S(2)}, u32[]{:S(2)}) %collective-permute-start.6) | collective-permute-done | bytes 16416 | tf_op jit(solution)/shard_map/ppermute | solution.py:19
  76.7 1.5 fusion.2
  78.6 2.3 %select_reduce_fusion = (f32[]{:T(128)}, f32[]{:T(128)}, f32[1,1,8,128,128]{4,3,2,1,0:T(8,128)S(1)}) fusion(f32[128,128]{1,0:T(8,128)S(1)} %bitcast.221, s32[128,128]{1,0:T(8,128)S(1)} %copy-done.6, s32[128,128]{1,0:T(8,128)S(1)} %bitcast.217, f32[1,1,8,128,128]{4,3,2,1,0:T(8,128)} %param.15, f32[1,1,8,128,128]{4,3,2,1,0:T(8,128)S(1)} %copy-done.2, ...), kind=kLoop, calls=%fused_computation.28 | loop fusion | flops 2883582 | bytes 2949128 | tf_op jit(solution)/shard_map/reduce_sum | solution.py:214
  80.9 38.6 %all-reduce.4 = (f32[]{:T(128)}, f32[]{:T(128)}) all-reduce(f32[]{:T(128)} %get-tuple-element.6, f32[]{:T(128)} %get-tuple-element.5), channel_id=1, replica_groups=mesh['blocks'=8,'lev'=4] {'blocks','lev'}, use_global_device_ids=true, to_apply=%region_1.2 | all-reduce | flops 2 | bytes 16 | tf_op jit(solution)/shard_map/psum | solution.py:215
  120.9 2.5 %subtract_select_fusion = f32[1,1,8,128,128]{4,3,2,1,0:T(8,128)S(1)} fusion(f32[1,1,8,128,128]{4,3,2,1,0:T(8,128)S(1)} %copy-done.2, f32[1,1,8,128,128]{4,3,2,1,0:T(8,128)S(1)} %get-tuple-element.11, f32[1,1,8,128,128]{4,3,2,1,0:T(8,128)S(1)} %copy.86, f32[1,1,8,127,128]{4,3,2,1,0:T(8,128)S(1)} %bitcast.225, f32[1,1,8,1,128]{4,3,2,1,0:T(1,128)S(1)} %bitcast.236, ...), kind=kLoop, calls=%fused_computation.27 | loop fusion | flops 5242880 | bytes 5701708 | tf_op jit(solution)/shard_map/jit(_where)/select_n | solution.py:216
  123.3 4.6 %copy.87 = f32[1,1,8,128,128]{2,4,3,1,0:T(8,128)} copy(f32[1,1,8,128,128]{4,3,2,1,0:T(8,128)S(1)} %subtract_select_fusion) | data formatting | bytes 1048576 | tf_op jit(solution)/shard_map/jit(_where)/select_n | solution.py:216
  128.0 1.8 %gather_fusion.5 = f32[128,8]{1,0:T(8,128)S(1)} fusion(f32[1,8,16384]{1,2,0:T(8,128)} %bitcast.210, s32[128]{0:T(128)S(1)} %get-tuple-element.46), kind=kCustom, calls=%fused_computation.5 | custom fusion | bytes 9216 | tf_op jit(solution)/shard_map/vmap()/gather | solution.py:125
  129.7 1.8 %gather_fusion.2 = f32[128,8]{1,0:T(8,128)S(1)} fusion(f32[1,8,16384]{1,2,0:T(8,128)} %bitcast.211, s32[128]{0:T(128)S(1)} %get-tuple-element.49), kind=kCustom, calls=%fused_computation.2 | custom fusion | bytes 9216 | tf_op jit(solution)/shard_map/vmap()/gather | solution.py:124
  131.6 7.7 %scatter_custom_fusion = f32[8,16384]{0,1:T(8,128)} fusion(f32[8,16384]{0,1:T(8,128)} %bitcast.212, s32[128]{0:T(128)} %get-tuple-element.50, f32[128,8]{1,0:T(8,128)S(1)} %gather_fusion.2, f32[128,8]{1,0:T(8,128)S(1)} %gather_fusion.5, f32[128]{0:T(128)S(1)} %copy-done.9, s32[128]{0:T(128)S(1)} %copy-done.12, f32[128]{0:T(128)S(1)} %copy-done.10, ...), kind=kCustom, calls=%fused_computation.47 | custom fusion | flops 6144 | bytes 534528 | tf_op jit(solution)/shard_map/vmap()/scatter | solution.py:130
  139.3 7.7 %scatter_custom_fusion.1 = f32[8,16384]{0,1:T(8,128)} fusion(f32[8,16384]{0,1:T(8,128)} %scatter_custom_fusion, s32[128]{0:T(128)} %get-tuple-element.45, f32[128,8]{1,0:T(8,128)S(1)} %gather_fusion.5, f32[128,8]{1,0:T(8,128)S(1)} %gather_fusion.2, f32[128]{0:T(128)S(1)} %copy-done.9, s32[128]{0:T(128)S(1)} %copy-done.12, f32[128]{0:T(128)S(1)} %copy-done.10, ...), kind=kCustom, calls=%fused_computation.45 | custom fusion | flops 6144 | bytes 534528 | tf_op jit(solution)/shard_map/vmap()/scatter | solution.py:131
  147.0 5.9 %copy.89 = f32[1,1,8,128,128]{4,3,2,1,0:T(8,128)} copy(f32[1,1,8,128,128]{2,4,3,1,0:T(8,128)} %bitcast.213) | data formatting | bytes 1048576 | tf_op jit(solution)/shard_map/vmap()/reshape | solution.py:132
  (86 shorter events, 20.4 us)
Async XLA Ops:
  0.0 54.3 %copy-start.2 = (f32[1,1,8,128,128]{4,3,2,1,0:T(8,128)S(1)}, f32[1,1,8,128,128]{4,3,2,1,0:T(8,128)}, u32[]{:S(2)}) copy-start(f32[1,1,8,128,128]{4,3,2,1,0:T(8,128)} %param.11) | copy-start | bytes 1572868
  0.0 47.8 %copy-start.4 = (f32[1,8,128,128]{3,2,1,0:T(8,128)S(1)}, f32[1,8,128,128]{3,2,1,0:T(8,128)}, u32[]{:S(2)}) copy-start(f32[1,8,128,128]{3,2,1,0:T(8,128)} %param.13) | copy-start | bytes 1572868
  2.8 10.5 %copy-start.7 = (f32[8,4,1,8,128]{4,3,2,1,0:T(8,128)}, f32[8,4,1,8,128]{4,3,2,1,0:T(8,128)S(1)}, u32[]{:S(2)}) copy-start(f32[8,4,1,8,128]{4,3,2,1,0:T(8,128)S(1)} %get-tuple-element.40) | copy-start | bytes 393220
  2.8 55.2 %collective-permute-start = (f32[1,4,1,8,128]{4,3,2,1,0:T(8,128)}, f32[1,4,1,8,128]{4,3,2,1,0:T(8,128)}, u32[]{:S(2)}, u32[]{:S(2)}) collective-permute-start(f32[1,4,1,8,128]{4,3,2,1,0:T(8,128)} %get-tuple-element.39), channel_id=1, source_target_pairs={{0,4},{4,8},{8,12},{12,16},{16,20},{20,24},{24,28},{28,0},{1,5},{5... | collective-permute-start | bytes 49160 | tf_op jit(solution)/shard_map/ppermute | solution.py:19
  3.3 55.0 %collective-permute-start.1 = (f32[1,4,1,8,128]{4,3,2,1,0:T(8,128)}, f32[1,4,1,8,128]{4,3,2,1,0:T(8,128)}, u32[]{:S(2)}, u32[]{:S(2)}) collective-permute-start(f32[1,4,1,8,128]{4,3,2,1,0:T(8,128)} %get-tuple-element.39), channel_id=1, source_target_pairs={{0,28},{4,0},{8,4},{12,8},{16,12},{20,16},{24,20},{28,24},{1,29},{... | collective-permute-start | bytes 49160 | tf_op jit(solution)/shard_map/ppermute | solution.py:24
  18.0 6.4 %copy-start.13 = (s32[128]{0:T(128)}, s32[128]{0:T(128)S(1)}, u32[]{:S(2)}) copy-start(s32[128]{0:T(128)S(1)} %gather_fusion) | copy-start | bytes 1540
  43.5 35.0 %copy-start = (s32[1,128,128]{2,1,0:T(8,128)S(1)}, s32[1,128,128]{2,1,0:T(8,128)}, u32[]{:S(2)}) copy-start(s32[1,128,128]{2,1,0:T(8,128)} %param.16) | copy-start | bytes 196612
  43.6 35.0 %copy-start.1 = (f32[1,128,128]{2,1,0:T(8,128)S(1)}, f32[1,128,128]{2,1,0:T(8,128)}, u32[]{:S(2)}) copy-start(f32[1,128,128]{2,1,0:T(8,128)} %param.17) | copy-start | bytes 196612
  46.3 74.6 %copy-start.3 = (f32[1,8,128,128]{3,2,1,0:T(8,128)S(1)}, f32[1,8,128,128]{3,2,1,0:T(8,128)}, u32[]{:S(2)}) copy-start(f32[1,8,128,128]{3,2,1,0:T(8,128)} %param.14) | copy-start | bytes 1572868
  46.6 0.6 copy-start.8
  50.0 28.5 %copy-start.5 = (f32[1,1,8,128,128]{4,2,3,1,0:T(8,128)S(1)}, f32[1,1,8,128,128]{4,2,3,1,0:T(8,128)}, u32[]{:S(2)}) copy-start(f32[1,1,8,128,128]{4,2,3,1,0:T(8,128)} %maximum_add_fusion.1) | copy-start | bytes 1572868
  53.5 25.0 %copy-start.6 = (s32[128,128]{1,0:T(8,128)S(1)}, s32[128,128]{1,0:T(8,128)}, u32[]{:S(2)}) copy-start(s32[128,128]{1,0:T(8,128)} %broadcast_add_fusion) | copy-start | bytes 196612
  57.9 6.2 %collective-permute-start.2 = (f32[1,4,1,8,128]{4,3,2,1,0:T(8,128)}, f32[1,4,1,8,128]{4,3,2,1,0:T(8,128)S(1)}, u32[]{:S(2)}, u32[]{:S(2)}) collective-permute-start(f32[1,4,1,8,128]{4,3,2,1,0:T(8,128)} %collective-permute-done), channel_id=1, source_target_pairs={{0,4},{4,8},{8,12},{12,16},{16,20},{20,24},{24,28},{28,0},{1,5},{5... | collective-permute-start | bytes 49160 | tf_op jit(solution)/shard_map/ppermute | solution.py:19
  58.3 5.8 %collective-permute-start.3 = (f32[1,4,1,8,128]{4,3,2,1,0:T(8,128)}, f32[1,4,1,8,128]{4,3,2,1,0:T(8,128)S(1)}, u32[]{:S(2)}, u32[]{:S(2)}) collective-permute-start(f32[1,4,1,8,128]{4,3,2,1,0:T(8,128)} %collective-permute-done.1), channel_id=1, source_target_pairs={{0,28},{4,0},{8,4},{12,8},{16,12},{20,16},{24,20},{28,24},{1,29},{... | collective-permute-start | bytes 49160 | tf_op jit(solution)/shard_map/ppermute | solution.py:24
  64.1 5.0 %collective-permute-start.4 = (f32[1,4,1,8,128]{4,3,2,1,0:T(8,128)S(1)}, f32[1,4,1,8,128]{4,3,2,1,0:T(8,128)S(1)}, u32[]{:S(2)}, u32[]{:S(2)}) collective-permute-start(f32[1,4,1,8,128]{4,3,2,1,0:T(8,128)S(1)} %collective-permute-done.2), channel_id=1, source_target_pairs={{0,4},{4,8},{8,12},{12,16},{16,20},{20,24},{24,28},{28,0},{1,5},{5... | collective-permute-start | bytes 49160 | tf_op jit(solution)/shard_map/ppermute | solution.py:19
  64.1 5.6 %collective-permute-start.5 = (f32[1,4,1,8,128]{4,3,2,1,0:T(8,128)S(1)}, f32[1,4,1,8,128]{4,3,2,1,0:T(8,128)S(1)}, u32[]{:S(2)}, u32[]{:S(2)}) collective-permute-start(f32[1,4,1,8,128]{4,3,2,1,0:T(8,128)S(1)} %collective-permute-done.3), channel_id=1, source_target_pairs={{0,28},{4,0},{8,4},{12,8},{16,12},{20,16},{24,20},{28,24},{1,29},{... | collective-permute-start | bytes 49160 | tf_op jit(solution)/shard_map/ppermute | solution.py:24
  69.1 5.0 %collective-permute-start.6 = (f32[1,4,1,8,128]{4,3,2,1,0:T(8,128)S(1)}, f32[1,4,1,8,128]{4,3,2,1,0:T(8,128)S(1)}, u32[]{:S(2)}, u32[]{:S(2)}) collective-permute-start(f32[1,4,1,8,128]{4,3,2,1,0:T(8,128)S(1)} %collective-permute-done.4), channel_id=1, source_target_pairs={{0,4},{4,8},{8,12},{12,16},{16,20},{20,24},{24,28},{28,0},{1,5},{5... | collective-permute-start | bytes 49160 | tf_op jit(solution)/shard_map/ppermute | solution.py:19
  75.9 45.0 %copy-start.14 = (pred[8]{0:T(512)(128)(4,1)S(1)}, pred[8]{0:T(512)(128)(4,1)}, u32[]{:S(2)}) copy-start(pred[8]{0:T(512)(128)(4,1)} %iota_compare_fusion.11) | copy-start | bytes 28
  78.5 53.0 %copy-start.9 = (f32[128]{0:T(128)S(1)}, f32[128]{0:T(128)}, u32[]{:S(2)}) copy-start(f32[128]{0:T(128)} %gather_fusion.1) | copy-start | bytes 1540
  78.6 53.0 %copy-start.10 = (f32[128]{0:T(128)S(1)}, f32[128]{0:T(128)}, u32[]{:S(2)}) copy-start(f32[128]{0:T(128)} %get-tuple-element.9) | copy-start | bytes 1540
  78.6 53.0 %copy-start.11 = (f32[128]{0:T(128)S(1)}, f32[128]{0:T(128)}, u32[]{:S(2)}) copy-start(f32[128]{0:T(128)} %get-tuple-element.10) | copy-start | bytes 1540
  78.6 53.0 %copy-start.12 = (s32[128]{0:T(128)S(1)}, s32[128]{0:T(128)}, u32[]{:S(2)}) copy-start(s32[128]{0:T(128)} %broadcast_add_fusion.1) | copy-start | bytes 1540
